TPU v7x, 128 devices: a whole 4x4x4 slice. The times are simulated.
128 devices in a mesh: sample: 8 (over x, core), gene: 4 (over y), cohort: 4 (over z).
Axes of the slice: x: 4, y: 4, z: 4, core: 2. Of those that a mesh axis runs over, the one named last changes fastest.
Arguments:
- dosage: bfloat16 [16384, 32768], P(('sample', 'cohort'), 'gene'), may hold values from 0 to 2
- covariates: bfloat16 [16384, 32], P(('sample', 'cohort')), may hold values from 0 to 2
- phenotype: bfloat16 [16384], P(('sample', 'cohort')), may hold values from -6 to 6
- sample_mask: int32 [16384], P(('sample', 'cohort')), may hold values 0 or 1
- variant_weight: float32 [32768], replicated, may hold values from 0.1 to 1
- bucket_owner: int32 [256], replicated, may hold values from 0 to 15, as said below
- variant_gene: int32 [32768], replicated, may hold values from -1 to 127, as said below
Outputs:
- gram_tiles: float32 [16, 16, 128, 128], P(('gene', 'cohort'), 'sample')
- rho_stats: float32 [8, 128], P(None, ('gene', 'cohort'))
- gene_trace: float32 [128], P(('gene', 'cohort'))
Inputs may be any that keep to these rules, and one draw needn't show every extreme that they name: `bucket_owner`: every owner holds exactly 16 buckets, at most 8 of them among the 64 buckets of one index of gene, and some owner exactly 8; of the buckets of one index of gene, exactly 16 belong to owners whose index leaves a given remainder on division by the size of the cohort axis. `variant_gene`: genes o * 8 to (o + 1) * 8 - 1 lie in the buckets of owner o, each in one or more whole buckets that are consecutive among that owner's buckets; all its buckets are full but its last, whose first 10 to 128 columns are live and the rest -1.
All inputs are finite; a program needn't handle non-finite values. No bound on the sum of `sample_mask` on one device may be relied on, other than what follows from the above.
Results may differ from a plain program's by a relative error of at most 0.0003.
Values may be sent and summed in bfloat16 or wider, within the bound.
No kernel may reach another device: no remote copies, remote signals or barrier semaphores. Data moves between devices by JAX's collectives and lax.ppermute only.
A program may use at most 128 MiB of HBM per device.

v0:
```python
import math
import jax
import jax.numpy as jnp
from jax import lax
from jax.sharding import PartitionSpec as P

BUCKET_WIDTH = 128
GENES_OWN = 8
RHO_GRID = (0.0, 0.01, 0.04, 0.09, 0.16, 0.25, 0.5, 1.0)


def solve_moments(factor, rhs):
    half = lax.linalg.triangular_solve(factor, rhs, left_side=True, lower=True)
    return lax.linalg.triangular_solve(factor, half, left_side=True, lower=True, transpose_a=True)


def inner_rows(first, second):
    return lax.dot_general(
        first, second, (((0,), (0,)), ((), ())), preferred_element_type=jnp.float32
    )


def block_rank(labels, group_count, label_count):
    onehot = (labels[:, None] == jnp.arange(label_count, dtype=jnp.int32)[None, :]).astype(
        jnp.int32
    )
    blocks = onehot.reshape(group_count, labels.shape[0] // group_count, label_count)
    return jnp.sum((jnp.cumsum(blocks, axis=1) - blocks) * blocks, axis=2).reshape(labels.shape[0])


def finish_slots(
    gram, cross, slot_bucket, moments, variant_weight, variant_gene, owner_here, sample_total
):
    cov_count = moments.shape[0]
    slot_count = gram.shape[0]
    span_width = gram.shape[1]
    factor = jnp.linalg.cholesky(moments[:, :cov_count])
    beta_hat = solve_moments(factor, moments[:, cov_count:])[:, 0]
    cov_cross = cross[:, :cov_count, :]
    raw_score = cross[:, cov_count, :]
    stacked = jnp.transpose(cov_cross, (1, 0, 2)).reshape(cov_count, slot_count * span_width)
    solved = solve_moments(factor, stacked).reshape(cov_count, slot_count, span_width)
    projected = jnp.einsum("bcj,cbk->bjk", cov_cross, solved, precision=lax.Precision.HIGHEST)
    scores = raw_score - jnp.einsum(
        "bcj,c->bj", cov_cross, beta_hat, precision=lax.Precision.HIGHEST
    )
    bucket_total = variant_gene.shape[0] // span_width
    weight_rows = jnp.where(variant_gene >= 0, variant_weight, 0.0).reshape(
        bucket_total, span_width
    )
    live_weight = jnp.take(weight_rows, slot_bucket, axis=0)
    tiles = live_weight[:, :, None] * live_weight[:, None, :] * (gram - projected) / sample_total
    zscore = (live_weight * scores / math.sqrt(sample_total)).reshape(slot_count * span_width)
    gene_rows = (
        jnp.take(variant_gene.reshape(bucket_total, span_width), slot_bucket, axis=0)
        - owner_here * GENES_OWN
    )
    member = (
        gene_rows.reshape(slot_count * span_width)[:, None]
        == jnp.arange(GENES_OWN, dtype=jnp.int32)[None, :]
    ).astype(jnp.float32)
    squares = jnp.dot(zscore * zscore, member, precision=lax.Precision.HIGHEST)
    burden_sum = jnp.dot(zscore, member, precision=lax.Precision.HIGHEST)
    diagonal = jnp.diagonal(tiles, axis1=1, axis2=2).reshape(slot_count * span_width)
    trace_sum = jnp.dot(diagonal, member, precision=lax.Precision.HIGHEST)
    return (tiles, squares, burden_sum, trace_sum)


def shards(dosage, covariates, phenotype, sample_mask, variant_weight, bucket_owner, variant_gene):
    gene_count = lax.axis_size("gene")
    cohort_count = lax.axis_size("cohort")
    sample_count = lax.axis_size("sample")
    owner_count = gene_count * cohort_count
    span_width = BUCKET_WIDTH
    sample_rows = dosage.shape[0]
    src_buckets = dosage.shape[1] // span_width
    total_buckets = bucket_owner.shape[0]
    held_slots = total_buckets // owner_count
    cap_slots = held_slots // 2
    share = held_slots // sample_count
    sample_total = sample_rows * sample_count * cohort_count
    cohort_here = lax.axis_index("cohort")
    owner_here = lax.axis_index("gene") * cohort_count + cohort_here
    sample_keep = sample_mask.astype(jnp.bfloat16)
    masked_cov = covariates * sample_keep[:, None]
    left_cols = jnp.concatenate([masked_cov, (phenotype * sample_keep)[:, None]], axis=1)
    moments = lax.psum(
        inner_rows(masked_cov, jnp.concatenate([covariates, phenotype[:, None]], axis=1)),
        ("sample", "cohort"),
    )
    masked_dosage = (dosage * sample_keep[:, None]).reshape(sample_rows, src_buckets, span_width)
    owner_ids = jnp.arange(owner_count, dtype=jnp.int32)
    onehot = (bucket_owner[:, None] == owner_ids[None, :]).astype(jnp.int32)
    owner_rank = jnp.sum((jnp.cumsum(onehot, axis=0) - onehot) * onehot, axis=1)
    pair_rank = block_rank(bucket_owner, gene_count, owner_count)
    source_start = lax.axis_index("gene") * src_buckets
    mine_owner = lax.dynamic_slice_in_dim(bucket_owner, source_start, src_buckets)
    mine_rank = lax.dynamic_slice_in_dim(pair_rank, source_start, src_buckets)
    own_key = jnp.where(bucket_owner == owner_here, owner_rank, held_slots)
    own_bucket = (
        jnp.zeros((held_slots,), jnp.int32)
        .at[own_key]
        .set(jnp.arange(total_buckets, dtype=jnp.int32), mode="drop")
    )
    own_source = own_bucket // src_buckets
    own_pair = jnp.take(pair_rank, own_bucket)
    cohort_ids = jnp.arange(cohort_count, dtype=jnp.int32)
    flat_index = (
        (own_source[None, :] * cohort_count + cohort_ids[:, None]) * cap_slots + own_pair[None, :]
    ).reshape(cohort_count * held_slots)
    send_from = (
        jnp.full((owner_count * cap_slots,), -1, jnp.int32)
        .at[mine_owner * cap_slots + mine_rank]
        .set(jnp.arange(src_buckets, dtype=jnp.int32))
    )
    send_pick = jnp.maximum(send_from, 0)
    cohort_left = lax.all_gather(left_cols[:, None, :], "cohort", axis=1, tiled=True)
    packed = (
        jnp.take(masked_dosage, send_pick, axis=1)
        * (send_from >= 0).astype(jnp.bfloat16)[None, :, None]
    )
    packed = packed.reshape(sample_rows, owner_count, cap_slots, span_width)
    arrived = lax.all_to_all(packed, ("gene", "cohort"), split_axis=1, concat_axis=1, tiled=True)
    arrived = arrived.reshape(sample_rows, owner_count * cap_slots, span_width)
    owned = jnp.take(arrived, flat_index, axis=1).reshape(
        sample_rows, cohort_count, held_slots, span_width
    )
    gram = jnp.einsum("schj,schk->hjk", owned, owned, preferred_element_type=jnp.float32)
    cross = jnp.einsum("sci,schk->hik", cohort_left, owned, preferred_element_type=jnp.float32)
    slot_start = lax.axis_index("sample") * share
    gram, cross = lax.psum((gram, cross), "sample")
    tiles, squares, burden_sum, trace_sum = finish_slots(
        gram, cross, own_bucket, moments, variant_weight, variant_gene, owner_here, sample_total
    )
    tiles = lax.dynamic_slice_in_dim(tiles, slot_start, share)
    rho_col = jnp.array(RHO_GRID, dtype=jnp.float32)[:, None]
    rho_stats = (
        (1.0 - rho_col) * squares[None, :] + rho_col * (burden_sum * burden_sum)[None, :]
    ) / span_width
    gene_trace = trace_sum / span_width
    return (tiles[None], rho_stats, gene_trace)


def solution(mesh):
    placed = (
        P(("sample", "cohort"), "gene"),
        P(("sample", "cohort"), None),
        P(("sample", "cohort")),
        P(("sample", "cohort")),
        P(),
        P(),
        P(),
    )
    return jax.shard_map(
        shards,
        mesh=mesh,
        in_specs=placed,
        out_specs=(
            P(("gene", "cohort"), "sample", None, None),
            P(None, ("gene", "cohort")),
            P(("gene", "cohort")),
        ),
        check_vma=False,
    )
```

profile of v0, /device:TPU:0, one launch (start us, length us, event | category | flops | bytes accessed | tf_op | source)
XLA Modules:
  0.0 636.7 jit_solution(13550545437215399836)
XLA Ops:
  7.2 0.8 eq.67
  7.9 0.1 fusion.23
  8.0 0.1 reduce_window_sum.28
  8.2 0.2 select_reduce_fusion
  8.4 0.1 reshape.218
  8.5 0.8 compare_select_fusion.3
  9.3 0.8 scatter_custom_fusion.1
  10.1 0.0 copy-start.4
  10.1 0.0 copy-start.5
  10.1 12.0 %copy.54 = bf16[512,8192]{0,1:T(8,128)(2,1)} copy(bf16[512,8192]{1,0:T(8,128)(2,1)} %param.8) | data formatting | bytes 16777216 | tf_op args[0]
  22.1 0.0 copy-done.4
  22.1 0.0 copy-done.5
  22.1 7.1 %broadcast_multiply_fusion = bf16[512,8192]{0,1:T(8,128)(2,1)} fusion(bf16[512,8192]{0,1:T(8,128)(2,1)} %copy.54, bf16[512]{0:T(512)(128)(2,1)S(1)} %get-tuple-element.9), kind=kLoop, calls=%fused_computation.14 | loop fusion | flops 4194304 | bytes 16778240 | tf_op jit(solution)/shard_map/mul | solution.py:91
  29.2 11.9 %copy.55 = bf16[512,64,128]{2,0,1:T(8,128)(2,1)} copy(bf16[512,64,128]{0,2,1:T(8,128)(2,1)} %bitcast.130) | data formatting | bytes 16777216 | tf_op jit(solution)/shard_map/reshape | solution.py:91
  41.1 0.1 reshape.226
  41.2 0.1 broadcast_in_dim.106
  41.3 11.5 %gather_fusion.2 = bf16[128,512,128]{2,1,0:T(8,128)(2,1)} fusion(bf16[512,64,128]{2,0,1:T(8,128)(2,1)} %copy.55, s32[1024]{0:T(1024)S(1)} %pad_clamp_fusion.1), kind=kCustom, calls=%fused_computation.2 | custom fusion | bytes 33554944 | tf_op jit(solution)/shard_map/jit(_take)/gather | solution.py:119
  52.8 14.2 %select_multiply_fusion = bf16[512,16,8,128]{3,0,2,1:T(8,128)(2,1)} fusion(bf16[512,16,8,128]{3,0,2,1:T(8,128)(2,1)} %bitcast.127, pred[16,8]{1,0:T(8,128)(4,1)S(1)} %broadcast_in_dim.106, bf16[16,8]{1,0:T(8,128)(2,1)S(1)} %reshape.226), kind=kLoop, calls=%fused_computation.8 | loop fusion | flops 16777216 | bytes 33554816 | tf_op jit(solution)/shard_map/mul | solution.py:119
  67.0 8.3 %all-to-all-start = ((bf16[512,16,8,128]{3,0,2,1:T(8,128)(2,1)}), bf16[512,16,8,128]{3,0,2,1:T(8,128)(2,1)}, u32[]{:S(2)}, u32[]{:S(2)}) async-start(bf16[512,16,8,128]{3,0,2,1:T(8,128)(2,1)} %select_multiply_fusion), calls=%async_computation | async-start | bytes 33554432 | tf_op jit(solution)/shard_map/all_to_all | solution.py:123
  75.4 0.0 all-reduce.3.cloned.1.call-start
  75.4 0.0 copy-done.3
  75.5 0.6 reduce-window.6
  76.1 0.2 slice_reduce_fusion
  76.3 0.1 fusion.31
  76.4 1.4 scatter_custom_fusion
  77.8 0.7 gather_fusion.1
  78.5 0.1 add.149
  78.6 0.0 copy-done.2
  78.6 160.0 %all-gather.1 = bf16[4,33,512]{2,1,0:T(8,128)(2,1)S(1)} all-gather(bf16[1,33,512]{2,1,0:T(8,128)(2,1)S(1)} %maximum_bitcast_fusion), channel_id=2, replica_groups=mesh['sample'=8,'gene'=4,'cohort'=4] {'cohort'}, dimensions={0}, use_global_device_ids=true | all-gather | bytes 168960 | tf_op jit(solution)/shard_map/all_gather | solution.py:117
  238.8 0.1 fusion.24
  238.9 197.3 %psum.23 = f32[32,33]{0,1:T(8,128)S(1)} all-reduce(f32[32,33]{0,1:T(8,128)S(1)} %fusion.24), channel_id=1, replica_groups=mesh['sample'=8,'gene'=4,'cohort'=4] {'sample','cohort'}, use_global_device_ids=true, to_apply=%region_9.10 | all-reduce | flops 1056 | bytes 8448 | tf_op jit(solution)/shard_map/psum | solution.py:87
  436.2 0.1 copy.61
  436.3 2.9 cholesky.16
  439.2 0.6 compare_reduce_fusion
  439.9 0.7 fusion.28
  440.5 2.4 custom-call.12
  443.0 0.0 copy-done.1
  443.0 0.6 gather_fusion
  443.6 0.6 gather_fusion.4
  444.2 0.0 all-to-all-done
  444.2 11.7 %gather_fusion.3 = bf16[64,512,128]{2,1,0:T(8,128)(2,1)} fusion(bf16[512,128,128]{2,0,1:T(8,128)(2,1)} %bitcast.6, s32[1024]{0:T(1024)S(1)} %pad_clamp_fusion), kind=kCustom, calls=%fused_computation.3 | custom fusion | bytes 16777472 | tf_op jit(solution)/shard_map/jit(_take)/gather | solution.py:125
  456.0 12.0 %copy.56 = bf16[512,64,128]{2,1,0:T(8,128)(2,1)} copy(bf16[512,64,128]{2,0,1:T(8,128)(2,1)} %bitcast.128) | data formatting | bytes 16777216 | tf_op jit(solution)/shard_map/jit(_take)/gather | solution.py:125
  467.9 7.4 %broadcast_select_fusion = bf16[512,4,16,128]{3,2,1,0:T(8,128)(2,1)} fusion(bf16[512,4,16,128]{3,2,1,0:T(8,128)(2,1)} %bitcast.129, pred[4,16]{1,0:T(4,128)(4,1)S(1)} %compare_and_fusion), kind=kLoop, calls=%fused_computation.9 | loop fusion | flops 4194304 | bytes 16777280 | tf_op jit(solution)/shard_map/jit(_take)/select_n | solution.py:125
  475.3 25.9 %fusion.4 = f32[16,128,128]{2,1,0:T(8,128)} fusion(bf16[512,4,16,128]{3,2,1,0:T(8,128)(2,1)} %broadcast_select_fusion), kind=kOutput, calls=%fused_computation.15 | convolution fusion | flops 1073741824 | bytes 9437184 | tf_op jit(solution)/shard_map/schj,schk->hjk/dot_general | solution.py:128
  501.2 8.8 %fusion.9 = f32[16,33,128]{2,1,0:T(8,128)} fusion(bf16[512,4,33,1]{0,2,1,3:T(8,128)(2,1)S(1)} %reshape.299, bf16[512,4,16,128]{3,2,1,0:T(8,128)(2,1)} %broadcast_select_fusion), kind=kOutput, calls=%fused_computation.19 | convolution fusion | flops 276824064 | bytes 8794112 | tf_op jit(solution)/shard_map/sci,schk->hik/dot_general | solution.py:129
  510.0 0.0 all-reduce.3.cloned.1.call-update
  510.0 0.1 convolution_bitcast_fusion.1
  510.2 0.1 convolution_bitcast_fusion
  510.3 0.1 subtract_bitcast_fusion
  510.4 101.9 %all-reduce.3.cloned.1.call-done = (f32[16,128,128]{2,1,0:T(8,128)}, f32[16,33,128]{2,1,0:T(8,128)}) async-done(((f32[16,128,128]{2,1,0:T(8,128)}, f32[16,33,128]{2,1,0:T(8,128)}), (f32[16,128,128]{2,1,0:T(8,128)}, f32[16,33,128]{2,1,0:T(8,128)})) %all-reduce.3.cloned.1.call-update) | async-done | bytes 1318928 | tf_op jit(solution)/shard_map/psum | solution.py:131
  612.3 0.8 slice.59
  613.1 1.4 fusion.17
  614.5 1.2 fusion.20
  615.7 0.4 fusion.33
  616.1 0.1 bitcast_multiply_fusion
  616.2 3.3 fusion.8
  619.5 4.6 copy.65
  624.1 1.8 gather_fusion.5
  625.9 0.1 copy.66
  626.0 1.1 fusion.12
  627.1 0.6 convolution_bitcast_fusion.4
  627.7 0.6 fusion.13
  628.3 0.7 dynamic-slice_bitcast_fusion
  628.9 0.7 add_multiply_fusion
  (37 shorter events, 0.3 us)
Async XLA Ops:
  10.1 12.0 %copy-start.4 = (bf16[512]{0:T(512)(128)(2,1)S(1)}, bf16[512]{0:T(512)(128)(2,1)}, u32[]{:S(2)}) copy-start(bf16[512]{0:T(512)(128)(2,1)} %param.10) | copy-start | bytes 3076
  10.1 12.0 %copy-start.5 = (s32[512]{0:T(512)S(1)}, s32[512]{0:T(512)}, u32[]{:S(2)}) copy-start(s32[512]{0:T(512)} %param.11) | copy-start | bytes 6148
  67.0 8.4 %copy-start.3 = (s32[256]{0:T(256)S(1)}, s32[256]{0:T(256)}, u32[]{:S(2)}) copy-start(s32[256]{0:T(256)} %param.13) | copy-start | bytes 3076
  67.0 11.6 %copy-start.2 = (bf16[512,32]{0,1:T(8,128)(2,1)S(1)}, bf16[512,32]{0,1:T(8,128)(2,1)}, u32[]{:S(2)}) copy-start(bf16[512,32]{0,1:T(8,128)(2,1)} %param.9) | copy-start | bytes 98308
  67.0 375.9 %copy-start = (s32[32768]{0:T(1024)S(1)}, s32[32768]{0:T(1024)}, u32[]{:S(2)}) copy-start(s32[32768]{0:T(1024)} %param.14) | copy-start | bytes 393220
  67.0 375.9 %copy-start.1 = (f32[32768]{0:T(1024)S(1)}, f32[32768]{0:T(1024)}, u32[]{:S(2)}) copy-start(f32[32768]{0:T(1024)} %param.12) | copy-start | bytes 393220
  67.0 377.2 %all-to-all-start = ((bf16[512,16,8,128]{3,0,2,1:T(8,128)(2,1)}), bf16[512,16,8,128]{3,0,2,1:T(8,128)(2,1)}, u32[]{:S(2)}, u32[]{:S(2)}) async-start(bf16[512,16,8,128]{3,0,2,1:T(8,128)(2,1)} %select_multiply_fusion), calls=%async_computation | async-start | bytes 33554432 | tf_op jit(solution)/shard_map/all_to_all | solution.py:123
  75.4 536.9 %all-reduce.3.cloned.1.call-start = ((), (), s32[]{:S(2)}) async-start(), calls=%async_computation.1 | async-start | bytes 2752512 | tf_op jit(solution)/shard_map/psum | solution.py:131
  510.0 119.0 %copy-start.6 = (f32[8]{0:T(128)S(1)}, f32[8]{0:T(128)}, u32[]{:S(2)}) copy-start(f32[8]{0:T(128)} %constant.200.clone) | copy-start | bytes 100
  510.0 119.0 %copy-start.7 = (f32[8]{0:T(128)S(1)}, f32[8]{0:T(128)}, u32[]{:S(2)}) copy-start(f32[8]{0:T(128)} %constant.202) | copy-start | bytes 100
Sparse Core Ops, SparseCore 0:
  510.1 102.1 all-reduce.2
where the time goes:
time: 643 us; the launch traced here: 637 us
  blocking collectives  357 us (56%)
  waiting for transfers between devices  102 us (16%)
  local copies, waits for them, and re-layouts  72.6 us (11%)
  matrix products  43.6 us (7%)
  other arithmetic  38.3 us (6%)
  between operations  14.6 us (2%)
  starting transfers between devices  8.38 us (1%)
    psum x1, blocking collectives, shards(): lax.psum(inner_rows(masked_cov, jnp.concatenate([covariates, phenotype[:,...  197 us
    all_gather x1, blocking collectives, shards(): lax.all_gather(left_cols[:, None, :], 'cohort', axis=1, tiled=True)  160 us
    psum x1, waiting for transfers between devices, shards(): gram, cross = lax.psum((gram, cross), 'sample')  102 us
    dot_general x1, matrix products, shards(): jnp.einsum('schj,schk->hjk', owned, owned, preferred_element_type=jnp.flo...  25.9 us
    gather x2, local copies, waits for them, and re-layouts, shards(): jnp.take(arrived, flat_index, axis=1)  23.7 us
    mul x2, other arithmetic, shards(): jnp.take(masked_dosage, send_pick, axis=1)  14.2 us
  transfers between devices with their start and end apart: 2, of which 1 were waited for; matrix products, arithmetic and copies ran while one was open for 2% of the time, Pallas kernels for 0%

commit v1 on v0

--- a/solution.py
+++ b/solution.py
@@ -84,10 +84,9 @@
     sample_keep = sample_mask.astype(jnp.bfloat16)
     masked_cov = covariates * sample_keep[:, None]
     left_cols = jnp.concatenate([masked_cov, (phenotype * sample_keep)[:, None]], axis=1)
-    moments = lax.psum(
-        inner_rows(masked_cov, jnp.concatenate([covariates, phenotype[:, None]], axis=1)),
-        ("sample", "cohort"),
-    )
+    moments = inner_rows(masked_cov, jnp.concatenate([covariates, phenotype[:, None]], axis=1))
+    for w in ("cohort", "sample"):
+        moments = jax.lax.psum(moments, w)
     masked_dosage = (dosage * sample_keep[:, None]).reshape(sample_rows, src_buckets, span_width)
     owner_ids = jnp.arange(owner_count, dtype=jnp.int32)
     onehot = (bucket_owner[:, None] == owner_ids[None, :]).astype(jnp.int32)

time: 643 us -> 535 us (0.83)
  blocking collectives: 357 us -> 251 us
    psum x1 -> x2, blocking collectives: 197 us -> 91.3 us  [shards(): moments = jax.lax.psum(moments, w)]
    psum x1, waiting for transfers between devices: 102 us -> 68.6 us  [shards(): gram, cross = lax.psum((gram, cross), 'sample')]
    all_to_all x1, waiting for transfers between devices: 0.01 us -> 30.6 us  [shards(): lax.all_to_all(packed, ('gene', 'cohort'), split_axis=1, concat_axis=1, t...]
  transfers between devices with their start and end apart: 2 -> 2, of which waited for: 1 -> 2; matrix products, arithmetic and copies ran while one was open for 2% -> 2% of each run, Pallas kernels for 0% -> 0%
where the time goes in v1:
time: 535 us; the launch traced here: 528 us
  blocking collectives  251 us (47%)
  waiting for transfers between devices  99.2 us (19%)
  local copies, waits for them, and re-layouts  72.6 us (14%)
  matrix products  43.6 us (8%)
  other arithmetic  38.3 us (7%)
  between operations  14.6 us (3%)
  starting transfers between devices  8.38 us (2%)
    all_gather x1, blocking collectives, shards(): lax.all_gather(left_cols[:, None, :], 'cohort', axis=1, tiled=True)  160 us
    psum x2, blocking collectives, shards(): moments = jax.lax.psum(moments, w)  91.3 us
    psum x1, waiting for transfers between devices, shards(): gram, cross = lax.psum((gram, cross), 'sample')  68.6 us
    all_to_all x1, waiting for transfers between devices, shards(): lax.all_to_all(packed, ('gene', 'cohort'), split_axis=1, concat_axis=1, t...  30.6 us
    dot_general x1, matrix products, shards(): jnp.einsum('schj,schk->hjk', owned, owned, preferred_element_type=jnp.flo...  25.9 us
    gather x2, local copies, waits for them, and re-layouts, shards(): jnp.take(arrived, flat_index, axis=1)  23.7 us
    mul x2, other arithmetic, shards(): jnp.take(masked_dosage, send_pick, axis=1)  14.2 us
    unnamed x18, local copies, waits for them, and re-layouts  12 us
  transfers between devices with their start and end apart: 2, of which 2 were waited for; matrix products, arithmetic and copies ran while one was open for 2% of the time, Pallas kernels for 0%

profile of v1, /device:TPU:0, one launch (start us, length us, event | category | flops | bytes accessed | tf_op | source)
XLA Modules:
  0.0 527.9 jit_solution(8980923891999409403)
XLA Ops:
  7.2 0.8 eq.67
  7.9 0.1 fusion.23
  8.0 0.1 reduce_window_sum.28
  8.2 0.2 select_reduce_fusion
  8.4 0.1 reshape.218
  8.5 0.8 compare_select_fusion.3
  9.3 0.8 scatter_custom_fusion.1
  10.1 0.0 copy-start.4
  10.1 0.0 copy-start.5
  10.1 12.0 %copy.54 = bf16[512,8192]{0,1:T(8,128)(2,1)} copy(bf16[512,8192]{1,0:T(8,128)(2,1)} %param.8) | data formatting | bytes 16777216 | tf_op args[0]
  22.1 0.0 copy-done.4
  22.1 0.0 copy-done.5
  22.1 7.1 %broadcast_multiply_fusion = bf16[512,8192]{0,1:T(8,128)(2,1)} fusion(bf16[512,8192]{0,1:T(8,128)(2,1)} %copy.54, bf16[512]{0:T(512)(128)(2,1)S(1)} %get-tuple-element.9), kind=kLoop, calls=%fused_computation.14 | loop fusion | flops 4194304 | bytes 16778240 | tf_op jit(solution)/shard_map/mul | solution.py:90
  29.2 11.9 %copy.55 = bf16[512,64,128]{2,0,1:T(8,128)(2,1)} copy(bf16[512,64,128]{0,2,1:T(8,128)(2,1)} %bitcast.130) | data formatting | bytes 16777216 | tf_op jit(solution)/shard_map/reshape | solution.py:90
  41.1 0.1 reshape.226
  41.2 0.1 broadcast_in_dim.106
  41.3 11.5 %gather_fusion.2 = bf16[128,512,128]{2,1,0:T(8,128)(2,1)} fusion(bf16[512,64,128]{2,0,1:T(8,128)(2,1)} %copy.55, s32[1024]{0:T(1024)S(1)} %pad_clamp_fusion.1), kind=kCustom, calls=%fused_computation.2 | custom fusion | bytes 33554944 | tf_op jit(solution)/shard_map/jit(_take)/gather | solution.py:118
  52.8 14.2 %select_multiply_fusion = bf16[512,16,8,128]{3,0,2,1:T(8,128)(2,1)} fusion(bf16[512,16,8,128]{3,0,2,1:T(8,128)(2,1)} %bitcast.127, pred[16,8]{1,0:T(8,128)(4,1)S(1)} %broadcast_in_dim.106, bf16[16,8]{1,0:T(8,128)(2,1)S(1)} %reshape.226), kind=kLoop, calls=%fused_computation.8 | loop fusion | flops 16777216 | bytes 33554816 | tf_op jit(solution)/shard_map/mul | solution.py:118
  67.0 8.3 %all-to-all-start = ((bf16[512,16,8,128]{3,0,2,1:T(8,128)(2,1)}), bf16[512,16,8,128]{3,0,2,1:T(8,128)(2,1)}, u32[]{:S(2)}, u32[]{:S(2)}) async-start(bf16[512,16,8,128]{3,0,2,1:T(8,128)(2,1)} %select_multiply_fusion), calls=%async_computation | async-start | bytes 33554432 | tf_op jit(solution)/shard_map/all_to_all | solution.py:122
  75.4 0.0 all-reduce.3.cloned.1.call-start
  75.4 0.0 copy-done.3
  75.5 0.6 reduce-window.6
  76.1 0.2 slice_reduce_fusion
  76.3 0.1 fusion.31
  76.4 1.4 scatter_custom_fusion
  77.8 0.7 gather_fusion.1
  78.5 0.1 add.151
  78.6 0.0 copy-done.2
  78.6 160.0 %all-gather.1 = bf16[4,33,512]{2,1,0:T(8,128)(2,1)S(1)} all-gather(bf16[1,33,512]{2,1,0:T(8,128)(2,1)S(1)} %maximum_bitcast_fusion), channel_id=2, replica_groups=mesh['sample'=8,'gene'=4,'cohort'=4] {'cohort'}, dimensions={0}, use_global_device_ids=true | all-gather | bytes 168960 | tf_op jit(solution)/shard_map/all_gather | solution.py:116
  238.8 0.1 fusion.24
  238.9 66.5 %psum.30 = f32[32,33]{0,1:T(8,128)S(1)} all-reduce(f32[32,33]{0,1:T(8,128)S(1)} %fusion.24), channel_id=1, replica_groups=mesh['sample'=8,'gene'=4,'cohort'=4] {'cohort'}, use_global_device_ids=true, to_apply=%region_9.10 | all-reduce | flops 1056 | bytes 8448 | tf_op jit(solution)/shard_map/psum | solution.py:89
  305.4 24.8 %psum.31 = f32[32,33]{0,1:T(8,128)S(1)} all-reduce(f32[32,33]{0,1:T(8,128)S(1)} %psum.30), channel_id=1, replica_groups=mesh['sample'=8,'gene'=4,'cohort'=4] {'sample'}, use_global_device_ids=true, to_apply=%region_10.11 | all-reduce | flops 1056 | bytes 8448 | tf_op jit(solution)/shard_map/psum | solution.py:89
  330.2 0.1 copy.61
  330.3 2.9 cholesky.16
  333.2 0.6 compare_reduce_fusion
  333.9 0.7 fusion.28
  334.5 2.4 custom-call.12
  337.0 0.6 gather_fusion
  337.6 0.6 gather_fusion.4
  338.2 30.6 %all-to-all-done = bf16[512,16,8,128]{3,0,2,1:T(8,128)(2,1)} async-done(((bf16[512,16,8,128]{3,0,2,1:T(8,128)(2,1)}), bf16[512,16,8,128]{3,0,2,1:T(8,128)(2,1)}, u32[]{:S(2)}, u32[]{:S(2)}) %all-to-all-start) | async-done | bytes 16777248 | tf_op jit(solution)/shard_map/all_to_all | solution.py:122
  368.8 11.7 %gather_fusion.3 = bf16[64,512,128]{2,1,0:T(8,128)(2,1)} fusion(bf16[512,128,128]{2,0,1:T(8,128)(2,1)} %bitcast.6, s32[1024]{0:T(1024)S(1)} %pad_clamp_fusion), kind=kCustom, calls=%fused_computation.3 | custom fusion | bytes 16777472 | tf_op jit(solution)/shard_map/jit(_take)/gather | solution.py:124
  380.5 12.0 %copy.56 = bf16[512,64,128]{2,1,0:T(8,128)(2,1)} copy(bf16[512,64,128]{2,0,1:T(8,128)(2,1)} %bitcast.128) | data formatting | bytes 16777216 | tf_op jit(solution)/shard_map/jit(_take)/gather | solution.py:124
  392.5 7.4 %broadcast_select_fusion = bf16[512,4,16,128]{3,2,1,0:T(8,128)(2,1)} fusion(bf16[512,4,16,128]{3,2,1,0:T(8,128)(2,1)} %bitcast.129, pred[4,16]{1,0:T(4,128)(4,1)S(1)} %compare_and_fusion), kind=kLoop, calls=%fused_computation.9 | loop fusion | flops 4194304 | bytes 16777280 | tf_op jit(solution)/shard_map/jit(_take)/select_n | solution.py:124
  399.9 25.9 %fusion.4 = f32[16,128,128]{2,1,0:T(8,128)} fusion(bf16[512,4,16,128]{3,2,1,0:T(8,128)(2,1)} %broadcast_select_fusion), kind=kOutput, calls=%fused_computation.15 | convolution fusion | flops 1073741824 | bytes 9437184 | tf_op jit(solution)/shard_map/schj,schk->hjk/dot_general | solution.py:127
  425.8 8.8 %fusion.9 = f32[16,33,128]{2,1,0:T(8,128)} fusion(bf16[512,4,33,1]{0,2,1,3:T(8,128)(2,1)S(1)} %reshape.299, bf16[512,4,16,128]{3,2,1,0:T(8,128)(2,1)} %broadcast_select_fusion), kind=kOutput, calls=%fused_computation.19 | convolution fusion | flops 276824064 | bytes 8794112 | tf_op jit(solution)/shard_map/sci,schk->hik/dot_general | solution.py:128
  434.6 0.0 all-reduce.3.cloned.1.call-update
  434.6 0.1 convolution_bitcast_fusion.1
  434.7 0.1 convolution_bitcast_fusion
  434.9 0.1 subtract_bitcast_fusion
  434.9 68.6 %all-reduce.3.cloned.1.call-done = (f32[16,128,128]{2,1,0:T(8,128)}, f32[16,33,128]{2,1,0:T(8,128)}) async-done(((f32[16,128,128]{2,1,0:T(8,128)}, f32[16,33,128]{2,1,0:T(8,128)}), (f32[16,128,128]{2,1,0:T(8,128)}, f32[16,33,128]{2,1,0:T(8,128)})) %all-reduce.3.cloned.1.call-update) | async-done | bytes 1318928 | tf_op jit(solution)/shard_map/psum | solution.py:130
  503.5 0.8 slice.59
  504.4 1.4 fusion.17
  505.7 1.2 fusion.20
  506.9 0.4 fusion.33
  507.3 0.1 bitcast_multiply_fusion
  507.4 3.3 fusion.8
  510.7 4.6 copy.65
  515.3 1.8 gather_fusion.5
  517.1 0.1 copy.66
  517.2 1.1 fusion.12
  518.3 0.6 convolution_bitcast_fusion.4
  518.9 0.6 fusion.13
  519.5 0.7 dynamic-slice_bitcast_fusion
  520.2 0.7 add_multiply_fusion
  (38 shorter events, 0.3 us)
Async XLA Ops:
  10.1 12.0 %copy-start.4 = (bf16[512]{0:T(512)(128)(2,1)S(1)}, bf16[512]{0:T(512)(128)(2,1)}, u32[]{:S(2)}) copy-start(bf16[512]{0:T(512)(128)(2,1)} %param.10) | copy-start | bytes 3076
  10.1 12.0 %copy-start.5 = (s32[512]{0:T(512)S(1)}, s32[512]{0:T(512)}, u32[]{:S(2)}) copy-start(s32[512]{0:T(512)} %param.11) | copy-start | bytes 6148
  67.0 8.4 %copy-start.3 = (s32[256]{0:T(256)S(1)}, s32[256]{0:T(256)}, u32[]{:S(2)}) copy-start(s32[256]{0:T(256)} %param.13) | copy-start | bytes 3076
  67.0 11.6 %copy-start.2 = (bf16[512,32]{0,1:T(8,128)(2,1)S(1)}, bf16[512,32]{0,1:T(8,128)(2,1)}, u32[]{:S(2)}) copy-start(bf16[512,32]{0,1:T(8,128)(2,1)} %param.9) | copy-start | bytes 98308
  67.0 269.9 %copy-start = (s32[32768]{0:T(1024)S(1)}, s32[32768]{0:T(1024)}, u32[]{:S(2)}) copy-start(s32[32768]{0:T(1024)} %param.14) | copy-start | bytes 393220
  67.0 269.9 %copy-start.1 = (f32[32768]{0:T(1024)S(1)}, f32[32768]{0:T(1024)}, u32[]{:S(2)}) copy-start(f32[32768]{0:T(1024)} %param.12) | copy-start | bytes 393220
  67.0 301.7 %all-to-all-start = ((bf16[512,16,8,128]{3,0,2,1:T(8,128)(2,1)}), bf16[512,16,8,128]{3,0,2,1:T(8,128)(2,1)}, u32[]{:S(2)}, u32[]{:S(2)}) async-start(bf16[512,16,8,128]{3,0,2,1:T(8,128)(2,1)} %select_multiply_fusion), calls=%async_computation | async-start | bytes 33554432 | tf_op jit(solution)/shard_map/all_to_all | solution.py:122
  75.4 428.1 %all-reduce.3.cloned.1.call-start = ((), (), s32[]{:S(2)}) async-start(), calls=%async_computation.1 | async-start | bytes 2752512 | tf_op jit(solution)/shard_map/psum | solution.py:130
  434.6 85.6 %copy-start.6 = (f32[8]{0:T(128)S(1)}, f32[8]{0:T(128)}, u32[]{:S(2)}) copy-start(f32[8]{0:T(128)} %constant.200.clone) | copy-start | bytes 100
  434.6 85.6 %copy-start.7 = (f32[8]{0:T(128)S(1)}, f32[8]{0:T(128)}, u32[]{:S(2)}) copy-start(f32[8]{0:T(128)} %constant.202) | copy-start | bytes 100
Sparse Core Ops, SparseCore 0:
  434.7 68.7 all-reduce.2
